TPU v7x, 32 devices: a whole 2x2x4 slice. The times are simulated.
32 devices in a mesh: sec: 4 (over y, x), gx: 4 (over z), gy: 2 (over core).
Axes of the slice: x: 2, y: 2, z: 4, core: 2. Of those that a mesh axis runs over, the one named last changes fastest.
Arguments:
- driving: float32 [3, 128, 256], P(None, 'gx', 'gy'), may hold values from -6 to 6
- rate_factor: float32 [3, 128, 256], P(None, 'gx', 'gy'), may hold values from 0.5 to 4
- friction_init: float32 [3, 128, 256], P(None, 'gx', 'gy'), may hold values from 0.2 to 2
- ice_mask: int32 [3, 128, 256], P(None, 'gx', 'gy'), may hold values 0 or 1
- grounded_mask: int32 [3, 128, 256], P(None, 'gx', 'gy'), may hold values 0 or 1
- melt: float32 [3, 128, 256], P(None, 'gx', 'gy'), may hold values from 0.1 to 1
- transmissivity: float32 [3, 128, 256], P(None, 'gx', 'gy'), may hold values from 0.5 to 5
- leakage: float32 [3, 128, 256], P(None, 'gx', 'gy'), may hold values from 0.05 to 0.5
- overburden: float32 [3, 128, 256], P(None, 'gx', 'gy'), may hold values from 0.5 to 2
- friction_scale: float32 [3, 128, 256], P(None, 'gx', 'gy'), may hold values from 0.5 to 4
Outputs:
- column_out: float32 [4, 3, 128, 256], P('sec', None, 'gx', 'gy')
All inputs are finite; a program needn't handle non-finite values. No bound on the sum of `ice_mask` or of `grounded_mask` on one device may be relied on, other than what follows from the above.
Results may differ from a plain program's by a relative error of at most 0.00002.
Values sent between devices are 32-bit elements; how exact they have to be, the bound alone decides.
A program may use at most 64 MiB of HBM per device.

v0:
```python
import jax
import jax.numpy as jnp
from jax import lax
from jax.sharding import PartitionSpec as P

LAYERS = 40
PICARD = 2
SWEEPS = 4
VERT = 4.0
FLOOR = 0.25
HEATING = 0.5


def extended(cells, sides, width):
    for axis, dim in sides:
        count = lax.axis_size(axis)
        ends = count - 1
        head = lax.slice_in_dim(cells, 0, width, axis=dim)
        tail = lax.slice_in_dim(cells, cells.shape[dim] - width, cells.shape[dim], axis=dim)
        cells = jnp.concatenate(
            [
                lax.ppermute(tail, axis, [(i, (i + 1) % count) for i in range(ends)]),
                cells,
                lax.ppermute(head, axis, [((i + 1) % count, i) for i in range(ends)]),
            ],
            axis=dim,
        )
    return cells


def ice_core(velocity, x_plus, x_minus, y_plus, y_minus, driving, rate_here, friction, icemask):
    layers = velocity.shape[0]
    vertical = jnp.concatenate([velocity[1:] - velocity[:-1], jnp.zeros_like(velocity[:1])], axis=0)
    strain = (
        vertical * vertical
        + 0.25 * (x_plus - x_minus) ** 2
        + 0.25 * (y_plus - y_minus) ** 2
        + FLOOR
    )
    viscous = rate_here * strain ** (-1.0 / 3.0)
    coupling = VERT * 0.5 * (viscous[:-1] + viscous[1:])
    right_side = driving + viscous * (x_plus + x_minus + y_plus + y_minus)
    ratios = []
    values = []
    for level_k in range(layers):
        pivot_k = 4.0 * viscous[level_k]
        term_k = right_side[level_k]
        if level_k < layers - 1:
            pivot_k = pivot_k + coupling[level_k]
        if level_k > 0:
            pivot_k = pivot_k + coupling[level_k - 1] - coupling[level_k - 1] * ratios[level_k - 1]
            term_k = term_k + coupling[level_k - 1] * values[level_k - 1]
        else:
            pivot_k = pivot_k + friction
        values.append(term_k / pivot_k)
        if level_k < layers - 1:
            ratios.append(coupling[level_k] / pivot_k)
    result = [values[-1]]
    for level_k in range(layers - 2, -1, -1):
        result.insert(0, values[level_k] + ratios[level_k] * result[0])
    return jnp.stack(result) * icemask


def neighbour_views(padded):
    return (padded[:, 2:, 1:-1], padded[:, :-2, 1:-1], padded[:, 1:-1, 2:], padded[:, 1:-1, :-2])


def sweep_padded(press_pad, trans_pad, leakage, source, inside):
    trans_centre = trans_pad[:, 1:-1, 1:-1]
    numerator = source
    denominator = leakage
    for trans_next, press_next in zip(neighbour_views(trans_pad), neighbour_views(press_pad)):
        face_weight = 0.5 * (trans_centre + trans_next)
        numerator = numerator + face_weight * press_next
        denominator = denominator + face_weight
    return jnp.where(inside > 0.5, numerator / (denominator + (1.0 - inside)), 0.0)


def water_solve(pressure, trans_eff, leakage, source):
    depth = SWEEPS
    stacked = jnp.stack([pressure, trans_eff, leakage, source, jnp.ones_like(pressure)])
    fields = extended(stacked, (("gx", 2), ("gy", 3)), depth)
    press_pad = fields[0]
    for sweep_i in range(SWEEPS):
        inner = sweep_i + 1
        trans_pad = fields[1][
            :, sweep_i : fields.shape[2] - sweep_i, sweep_i : fields.shape[3] - sweep_i
        ]
        leak_in = fields[2][:, inner : fields.shape[2] - inner, inner : fields.shape[3] - inner]
        source_in = fields[3][:, inner : fields.shape[2] - inner, inner : fields.shape[3] - inner]
        inside = fields[4][:, inner : fields.shape[2] - inner, inner : fields.shape[3] - inner]
        press_pad = sweep_padded(press_pad, trans_pad, leak_in, source_in, inside)
    return press_pad


def on_device(
    driving,
    rate_factor,
    friction_init,
    ice_mask,
    grounded_mask,
    melt,
    transmissivity,
    leakage,
    overburden,
    friction_scale,
):
    sectors = lax.axis_size("sec") - 1
    section = lax.axis_index("sec")
    is_ice = section < sectors
    strip_index = jnp.minimum(section, sectors - 1)

    def take_strip(values_in):
        return lax.dynamic_index_in_dim(values_in, strip_index, 0, keepdims=False)

    driving_here = take_strip(driving)
    rate_here = take_strip(rate_factor)
    icemask = take_strip(ice_mask).astype(jnp.float32)
    grounded = grounded_mask.astype(jnp.float32)
    friction_all = friction_init * grounded
    friction_here = take_strip(friction_all)
    width_x = driving.shape[1]
    width_y = driving.shape[2]
    velocity = jnp.zeros((LAYERS, width_x, width_y), jnp.float32)
    pressure = overburden
    for picard in range(PICARD):
        padded = extended(velocity, (("gx", 1), ("gy", 2)), 1)
        x_plus, x_minus, y_plus, y_minus = neighbour_views(padded)
        old_velocity = velocity
        fric_now = friction_here
        velocity = lax.cond(
            is_ice,
            lambda: ice_core(
                old_velocity,
                x_plus,
                x_minus,
                y_plus,
                y_minus,
                driving_here,
                rate_here,
                fric_now,
                icemask,
            ),
            lambda: jnp.zeros_like(old_velocity),
        )
        basal_rows = lax.all_gather(velocity[:1], "sec", axis=0, tiled=True)
        sliding = basal_rows[:sectors]
        squared = sliding * sliding
        trans_eff = transmissivity * (1.0 + squared / (1.0 + squared))
        source = melt + HEATING * friction_all * squared
        pressure = water_solve(pressure, trans_eff, leakage, source)
        friction_all = friction_scale * pressure * grounded
        friction_here = take_strip(friction_all)
    ice_stack = jnp.stack([velocity[-1], velocity[0], friction_here])
    column_out = jnp.where(is_ice, ice_stack, pressure)
    return column_out[None]


def solution(mesh):
    in_specs = (
        P(None, "gx", "gy"),
        P(None, "gx", "gy"),
        P(None, "gx", "gy"),
        P(None, "gx", "gy"),
        P(None, "gx", "gy"),
        P(None, "gx", "gy"),
        P(None, "gx", "gy"),
        P(None, "gx", "gy"),
        P(None, "gx", "gy"),
        P(None, "gx", "gy"),
    )
    out_specs = P("sec", None, "gx", "gy")
    return jax.shard_map(
        on_device, mesh=mesh, in_specs=in_specs, out_specs=out_specs, check_vma=False
    )
```

profile of v0, /device:TPU:0, one launch (start us, length us, event | category | flops | bytes accessed | tf_op | source)
XLA Modules:
  0.0 93.6 jit_solution(11888425895050816554)
XLA Ops:
  0.0 1.3 %collective-permute-start = (f32[40,1,128]{2,0,1:T(8,128)S(1)}, f32[40,1,128]{2,0,1:T(8,128)S(1)}, u32[]{:S(2)}, u32[]{:S(2)}) collective-permute-start(f32[40,1,128]{2,0,1:T(8,128)S(1)} %broadcast.6507), channel_id=1, source_target_pairs={{2,0},{4,2},{6,4},{3,1},{5,3},{7,5},{10,8},{12,10},{14,12},{11,9},... | collective-permute-start | bytes 61448 | tf_op jit(solution)/shard_map/ppermute | solution.py:24
  1.3 5.6 %collective-permute-start.1 = (f32[40,1,128]{2,0,1:T(8,128)S(1)}, f32[40,1,128]{2,0,1:T(8,128)S(1)}, u32[]{:S(2)}, u32[]{:S(2)}) collective-permute-start(f32[40,1,128]{2,0,1:T(8,128)S(1)} %broadcast.6507), channel_id=1, source_target_pairs={{0,2},{2,4},{4,6},{1,3},{3,5},{5,7},{8,10},{10,12},{12,14},{9,11},... | collective-permute-start | bytes 61448 | tf_op jit(solution)/shard_map/ppermute | solution.py:22
  6.9 0.8 bitcast_dynamic-update-slice_fusion.5
  7.7 0.8 convert_multiply_fusion
  8.5 0.7 dynamic-slice_bitcast_fusion
  9.9 1.3 %collective-permute-start.2 = (f32[40,34,1]{0,2,1:T(1,128)S(1)}, f32[40,34,1]{0,2,1:T(1,128)S(1)}, u32[]{:S(2)}, u32[]{:S(2)}) collective-permute-start(f32[40,34,1]{0,2,1:T(1,128)S(1)} %copy.56), channel_id=1, source_target_pairs={{1,0},{3,2},{5,4},{7,6},{9,8},{11,10},{13,12},{15,14},{17,16},{19,... | collective-permute-start | bytes 16328 | tf_op jit(solution)/shard_map/ppermute | solution.py:24
  11.5 3.0 %collective-permute-start.3 = (f32[40,34,1]{0,2,1:T(1,128)S(1)}, f32[40,34,1]{0,2,1:T(1,128)S(1)}, u32[]{:S(2)}, u32[]{:S(2)}) collective-permute-start(f32[40,34,1]{0,2,1:T(1,128)S(1)} %copy.57), channel_id=1, source_target_pairs={{0,1},{2,3},{4,5},{6,7},{8,9},{10,11},{12,13},{14,15},{16,17},{18,... | collective-permute-start | bytes 16328 | tf_op jit(solution)/shard_map/ppermute | solution.py:22
  14.6 0.7 convert_bitcast_fusion
  15.9 0.4 maximum_maximum_fusion.1
  16.4 3.6 %conditional.2 = (f32[40,32,128]{2,1,0:T(8,128)S(1)}) conditional(s32[]{:T(128)} %convert_element_type.13, () %tuple.32, (f32[32,128]{1,0:T(8,128)S(1)}, f32[32,128]{1,0:T(8,128)S(1)}, f32[40,1,128]{2,0,1:T(8,128)S(1)}, f32[40,1,128]{2,0,1:T(8,128)S(1)}, f32[40,34,129]{2,0,1:T(8,128)S(1)}, /*index=5*/f32[40,34,129]{2,0,1:T(8,128)S(1)}, ...), branch_computations={%region_0.1_spmd, %region_1.2_spmd} | conditional | flops 5099559 | bytes 16611208 | solution.py:131
  16.4 0.5 copy.47
  16.9 0.5 copy.48
  17.4 1.2 %multiply_add_fusion = (f32[40,32,128]{2,1,0:T(8,128)S(1)}, f32[40,32,128]{2,1,0:T(8,128)S(1)}) fusion(f32[40,34,129]{2,1,0:T(8,128)S(1)} %copy.48, f32[40,34,129]{2,1,0:T(8,128)S(1)} %copy.47, f32[40,1,128]{2,1,0:T(1,128)S(1)} %bitcast.49, f32[40,1,128]{2,1,0:T(1,128)S(1)} %bitcast.50, f32[32,128]{1,0:T(8,128)S(1)} %get-tuple-element.145, ...), kind=kLoop, calls=%fused_computation.2 | loop fusion | flops 2457600 | bytes 2695328 | tf_op jit(solution)/shard_map/cond/branch_1_fun/add | solution.py:42
  20.1 0.6 copy.49
  20.7 1.3 %collective-permute-start.4 = (f32[40,1,128]{0,2,1:T(8,128)S(1)}, f32[40,1,128]{0,2,1:T(8,128)S(1)}, u32[]{:S(2)}, u32[]{:S(2)}) collective-permute-start(f32[40,1,128]{0,2,1:T(8,128)S(1)} %get-tuple-element.434), channel_id=1, source_target_pairs={{2,0},{4,2},{6,4},{3,1},{5,3},{7,5},{10,8},{12,10},{14,12},{11,9},... | collective-permute-start | bytes 61448 | tf_op jit(solution)/shard_map/ppermute | solution.py:24
  22.0 4.6 %collective-permute-start.5 = (f32[40,1,128]{0,2,1:T(8,128)S(1)}, f32[40,1,128]{0,2,1:T(8,128)S(1)}, u32[]{:S(2)}, u32[]{:S(2)}) collective-permute-start(f32[40,1,128]{0,2,1:T(8,128)S(1)} %get-tuple-element.433), channel_id=1, source_target_pairs={{0,2},{2,4},{4,6},{1,3},{3,5},{5,7},{8,10},{10,12},{12,14},{9,11},... | collective-permute-start | bytes 61448 | tf_op jit(solution)/shard_map/ppermute | solution.py:22
  26.6 8.7 %all_gather.6 = f32[4,32,128]{2,1,0:T(8,128)S(1)} all-gather(f32[1,32,128]{2,1,0:T(8,128)S(1)} %slice.2411), channel_id=1, replica_groups=mesh['sec'=4,'gx'=4,'gy'=2] {'sec'}, dimensions={0}, use_global_device_ids=true | all-gather | bytes 81920 | tf_op jit(solution)/shard_map/all_gather | solution.py:146
  35.4 3.5 %collective-permute-start.8 = (f32[5,3,4,128]{3,2,1,0:T(4,128)S(1)}, f32[5,3,4,128]{3,2,1,0:T(4,128)S(1)}, u32[]{:S(2)}, u32[]{:S(2)}) collective-permute-start(f32[5,3,4,128]{3,2,1,0:T(4,128)S(1)} %get-tuple-element.457), channel_id=1, source_target_pairs={{0,2},{2,4},{4,6},{1,3},{3,5},{5,7},{8,10},{10,12},{12,14},{9,11},... | collective-permute-start | bytes 92168 | tf_op jit(solution)/shard_map/ppermute | solution.py:22
  39.0 1.3 %collective-permute-start.9 = (f32[5,3,4,128]{3,2,1,0:T(4,128)S(1)}, f32[5,3,4,128]{3,2,1,0:T(4,128)S(1)}, u32[]{:S(2)}, u32[]{:S(2)}) collective-permute-start(f32[5,3,4,128]{3,2,1,0:T(4,128)S(1)} %get-tuple-element.458), channel_id=1, source_target_pairs={{2,0},{4,2},{6,4},{3,1},{5,3},{7,5},{10,8},{12,10},{14,12},{11,9},... | collective-permute-start | bytes 92168 | tf_op jit(solution)/shard_map/ppermute | solution.py:24
  40.3 0.6 pad_maximum_fusion.9
  40.9 1.3 %collective-permute-start.6 = (f32[40,34,1]{0,2,1:T(1,128)}, f32[40,34,1]{0,2,1:T(1,128)S(1)}, u32[]{:S(2)}, u32[]{:S(2)}) collective-permute-start(f32[40,34,1]{0,2,1:T(1,128)} %get-tuple-element.432), channel_id=1, source_target_pairs={{1,0},{3,2},{5,4},{7,6},{9,8},{11,10},{13,12},{15,14},{17,16},{19,... | collective-permute-start | bytes 16328 | tf_op jit(solution)/shard_map/ppermute | solution.py:24
  42.2 3.6 %collective-permute-start.7 = (f32[40,34,1]{0,2,1:T(1,128)}, f32[40,34,1]{0,2,1:T(1,128)}, u32[]{:S(2)}, u32[]{:S(2)}) collective-permute-start(f32[40,34,1]{0,2,1:T(1,128)} %get-tuple-element.431), channel_id=1, source_target_pairs={{0,1},{2,3},{4,5},{6,7},{8,9},{10,11},{12,13},{14,15},{16,17},{18,... | collective-permute-start | bytes 16328 | tf_op jit(solution)/shard_map/ppermute | solution.py:22
  46.0 1.3 %pad_maximum_fusion.3 = (f32[40,33,128]{2,1,0:T(8,128)}, f32[40,33,128]{2,1,0:T(8,128)}) fusion(f32[40,32,128]{2,1,0:T(8,128)S(1)} %get-tuple-element.465, f32[40,1,128]{2,1,0:T(1,128)S(1)} %copy.52, f32[40,1,128]{2,1,0:T(1,128)S(1)} %copy.50), kind=kLoop, calls=%fused_computation.727 | loop fusion | flops 337920 | bytes 2048000 | tf_op jit(solution)/shard_map/concatenate | solution.py:20
  47.5 1.3 %collective-permute-start.10 = (f32[5,3,40,4]{3,2,1,0:T(8,128)S(1)}, f32[5,3,40,4]{3,2,1,0:T(8,128)S(1)}, u32[]{:S(2)}, u32[]{:S(2)}) collective-permute-start(f32[5,3,40,4]{3,2,1,0:T(8,128)S(1)} %get-tuple-element.453), channel_id=1, source_target_pairs={{0,1},{2,3},{4,5},{6,7},{8,9},{10,11},{12,13},{14,15},{16,17},{18,... | collective-permute-start | bytes 28808 | tf_op jit(solution)/shard_map/ppermute | solution.py:22
  48.8 1.3 %collective-permute-start.11 = (f32[5,3,40,4]{3,2,1,0:T(8,128)S(1)}, f32[5,3,40,4]{3,2,1,0:T(8,128)S(1)}, u32[]{:S(2)}, u32[]{:S(2)}) collective-permute-start(f32[5,3,40,4]{3,2,1,0:T(8,128)S(1)} %get-tuple-element.454), channel_id=1, source_target_pairs={{1,0},{3,2},{5,4},{7,6},{9,8},{11,10},{13,12},{15,14},{17,16},{19,... | collective-permute-start | bytes 28808 | tf_op jit(solution)/shard_map/ppermute | solution.py:24
  50.1 3.3 %maximum_maximum_fusion = (f32[40,34,129]{0,2,1:T(8,128)}, f32[40,34,129]{0,2,1:T(8,128)}) fusion(f32[40,1,128]{0,2,1:T(8,128)S(1)} %collective-permute-done.4, f32[40,32,128]{0,2,1:T(8,128)S(1)} %copy.49, f32[40,1,128]{0,2,1:T(8,128)S(1)} %collective-permute-done.5, f32[40,34,1]{0,2,1:T(1,128)} %collective-permute-done.7, ...), kind=kLoop, calls=%fused_computation.723 | loop fusion | flops 1052640 | bytes 2110720 | tf_op jit(solution)/shard_map/concatenate | solution.py:20
  53.4 0.4 pad_maximum_fusion.5
  53.8 0.4 fusion.389
  54.3 0.4 fusion.376
  54.7 0.4 fusion.363
  55.4 0.6 copy-done
  56.0 12.4 %conditional.3 = (f32[1,32,128]{2,1,0:T(8,128)S(1)}, f32[1,32,128]{2,1,0:T(8,128)S(1)}) conditional(s32[]{:T(128)} %convert_element_type.13, () %tuple.31, (f32[32,128]{1,0:T(8,128)S(1)}, f32[32,128]{1,0:T(8,128)S(1)}, f32[40,32,128]{2,1,0:T(8,128)S(1)}, f32[40,33,128]{2,1,0:T(8,128)}, f32[40,33,128]{2,1,0:T(8,128)}, ...), branch_computations={%region_2.3_spmd, %region_3.4_spmd} | conditional | flops 5423103 | bytes 25908556 | solution.py:131
  56.0 4.1 %copy.54 = f32[40,34,129]{2,1,0:T(8,128)} copy(f32[40,34,129]{0,2,1:T(8,128)} %get-tuple-element.220) | data formatting | bytes 1403520 | tf_op jit(solution)/shard_map
  60.1 2.6 %copy.55 = f32[40,34,129]{2,1,0:T(8,128)} copy(f32[40,34,129]{0,2,1:T(8,128)S(1)} %get-tuple-element.221) | data formatting | bytes 1403520 | tf_op jit(solution)/shard_map
  62.7 1.1 %copy-done.1 = f32[40,33,128]{2,1,0:T(8,128)S(1)} copy-done((f32[40,33,128]{2,1,0:T(8,128)S(1)}, f32[40,33,128]{2,1,0:T(8,128)}, u32[]{:S(2)}) %copy-start.1) | copy-done | bytes 675864 | tf_op jit(solution)/shard_map/cond
  64.0 2.9 %multiply_add_fusion.39 = (f32[40,32,128]{2,1,0:T(8,128)S(1)}, f32[40,32,128]{2,1,0:T(8,128)S(1)}) fusion(f32[40,34,129]{2,1,0:T(8,128)} %copy.55, f32[40,34,129]{2,1,0:T(8,128)} %copy.54, f32[40,33,128]{2,1,0:T(8,128)S(1)} %copy-done.1, f32[40,33,128]{2,1,0:T(8,128)S(1)} %copy-done.2, f32[32,128]{1,0:T(8,128)S(1)} %get-tuple-element.154, ...), kind=kLoop, calls=%fused_computation.362 | loop fusion | flops 2621440 | bytes 4603904 | tf_op jit(solution)/shard_map/cond/branch_1_fun/add | solution.py:42
  68.4 7.2 %all_gather.7 = f32[4,32,128]{2,1,0:T(8,128)S(1)} all-gather(f32[1,32,128]{2,1,0:T(8,128)S(1)} %get-tuple-element.167), channel_id=1, replica_groups=mesh['sec'=4,'gx'=4,'gy'=2] {'sec'}, dimensions={0}, use_global_device_ids=true | all-gather | bytes 81920 | tf_op jit(solution)/shard_map/all_gather | solution.py:146
  75.7 4.5 %collective-permute-start.12 = (f32[5,3,4,128]{3,2,1,0:T(4,128)S(1)}, f32[5,3,4,128]{3,2,1,0:T(4,128)S(1)}, u32[]{:S(2)}, u32[]{:S(2)}) collective-permute-start(f32[5,3,4,128]{3,2,1,0:T(4,128)S(1)} %get-tuple-element.455), channel_id=1, source_target_pairs={{0,2},{2,4},{4,6},{1,3},{3,5},{5,7},{8,10},{10,12},{12,14},{9,11},... | collective-permute-start | bytes 92168 | tf_op jit(solution)/shard_map/ppermute | solution.py:22
  80.2 1.3 %collective-permute-start.13 = (f32[5,3,4,128]{3,2,1,0:T(4,128)S(1)}, f32[5,3,4,128]{3,2,1,0:T(4,128)S(1)}, u32[]{:S(2)}, u32[]{:S(2)}) collective-permute-start(f32[5,3,4,128]{3,2,1,0:T(4,128)S(1)} %get-tuple-element.456), channel_id=1, source_target_pairs={{2,0},{4,2},{6,4},{3,1},{5,3},{7,5},{10,8},{12,10},{14,12},{11,9},... | collective-permute-start | bytes 92168 | tf_op jit(solution)/shard_map/ppermute | solution.py:24
  81.8 4.2 %collective-permute-done.13 = f32[5,3,4,128]{3,2,1,0:T(4,128)S(1)} collective-permute-done((f32[5,3,4,128]{3,2,1,0:T(4,128)S(1)}, f32[5,3,4,128]{3,2,1,0:T(4,128)S(1)}, u32[]{:S(2)}, u32[]{:S(2)}) %collective-permute-start.13) | collective-permute-done | bytes 30752 | tf_op jit(solution)/shard_map/ppermute | solution.py:24
  86.2 1.3 %collective-permute-start.14 = (f32[5,3,40,4]{3,2,1,0:T(8,128)S(1)}, f32[5,3,40,4]{3,2,1,0:T(8,128)S(1)}, u32[]{:S(2)}, u32[]{:S(2)}) collective-permute-start(f32[5,3,40,4]{3,2,1,0:T(8,128)S(1)} %get-tuple-element.451), channel_id=1, source_target_pairs={{0,1},{2,3},{4,5},{6,7},{8,9},{10,11},{12,13},{14,15},{16,17},{18,... | collective-permute-start | bytes 28808 | tf_op jit(solution)/shard_map/ppermute | solution.py:22
  87.5 1.3 %collective-permute-start.15 = (f32[5,3,40,4]{3,2,1,0:T(8,128)S(1)}, f32[5,3,40,4]{3,2,1,0:T(8,128)S(1)}, u32[]{:S(2)}, u32[]{:S(2)}) collective-permute-start(f32[5,3,40,4]{3,2,1,0:T(8,128)S(1)} %get-tuple-element.452), channel_id=1, source_target_pairs={{1,0},{3,2},{5,4},{7,6},{9,8},{11,10},{13,12},{15,14},{17,16},{19,... | collective-permute-start | bytes 28808 | tf_op jit(solution)/shard_map/ppermute | solution.py:24
  88.9 2.2 %collective-permute-done.15 = f32[5,3,40,4]{3,2,1,0:T(8,128)S(1)} collective-permute-done((f32[5,3,40,4]{3,2,1,0:T(8,128)S(1)}, f32[5,3,40,4]{3,2,1,0:T(8,128)S(1)}, u32[]{:S(2)}, u32[]{:S(2)}) %collective-permute-start.15) | collective-permute-done | bytes 9632 | tf_op jit(solution)/shard_map/ppermute | solution.py:24
  91.0 0.4 pad_maximum_fusion.6
  91.5 0.4 fusion.347
  91.9 0.4 fusion.334
  92.3 0.4 fusion.321
  93.0 0.6 fusion.436
  (155 shorter events, 5.6 us)
Async XLA Ops:
  0.0 9.3 %collective-permute-start = (f32[40,1,128]{2,0,1:T(8,128)S(1)}, f32[40,1,128]{2,0,1:T(8,128)S(1)}, u32[]{:S(2)}, u32[]{:S(2)}) collective-permute-start(f32[40,1,128]{2,0,1:T(8,128)S(1)} %broadcast.6507), channel_id=1, source_target_pairs={{2,0},{4,2},{6,4},{3,1},{5,3},{7,5},{10,8},{12,10},{14,12},{11,9},... | collective-permute-start | bytes 61448 | tf_op jit(solution)/shard_map/ppermute | solution.py:24
  1.3 8.0 %collective-permute-start.1 = (f32[40,1,128]{2,0,1:T(8,128)S(1)}, f32[40,1,128]{2,0,1:T(8,128)S(1)}, u32[]{:S(2)}, u32[]{:S(2)}) collective-permute-start(f32[40,1,128]{2,0,1:T(8,128)S(1)} %broadcast.6507), channel_id=1, source_target_pairs={{0,2},{2,4},{4,6},{1,3},{3,5},{5,7},{8,10},{10,12},{12,14},{9,11},... | collective-permute-start | bytes 61448 | tf_op jit(solution)/shard_map/ppermute | solution.py:22
  9.9 5.4 %collective-permute-start.2 = (f32[40,34,1]{0,2,1:T(1,128)S(1)}, f32[40,34,1]{0,2,1:T(1,128)S(1)}, u32[]{:S(2)}, u32[]{:S(2)}) collective-permute-start(f32[40,34,1]{0,2,1:T(1,128)S(1)} %copy.56), channel_id=1, source_target_pairs={{1,0},{3,2},{5,4},{7,6},{9,8},{11,10},{13,12},{15,14},{17,16},{19,... | collective-permute-start | bytes 16328 | tf_op jit(solution)/shard_map/ppermute | solution.py:24
  11.5 4.1 %collective-permute-start.3 = (f32[40,34,1]{0,2,1:T(1,128)S(1)}, f32[40,34,1]{0,2,1:T(1,128)S(1)}, u32[]{:S(2)}, u32[]{:S(2)}) collective-permute-start(f32[40,34,1]{0,2,1:T(1,128)S(1)} %copy.57), channel_id=1, source_target_pairs={{0,1},{2,3},{4,5},{6,7},{8,9},{10,11},{12,13},{14,15},{16,17},{18,... | collective-permute-start | bytes 16328 | tf_op jit(solution)/shard_map/ppermute | solution.py:22
  20.0 15.3 %copy-start.5 = (f32[3,32,128]{2,1,0:T(8,128)S(1)}, f32[3,32,128]{2,1,0:T(8,128)}, u32[]{:S(2)}) copy-start(f32[3,32,128]{2,1,0:T(8,128)} %param.20) | copy-start | bytes 147460
  20.0 15.3 %copy-start.4 = (f32[3,32,128]{2,1,0:T(8,128)S(1)}, f32[3,32,128]{2,1,0:T(8,128)}, u32[]{:S(2)}) copy-start(f32[3,32,128]{2,1,0:T(8,128)} %param.21) | copy-start | bytes 147460
  20.1 15.3 %copy-start.6 = (f32[3,32,128]{2,1,0:T(8,128)S(1)}, f32[3,32,128]{2,1,0:T(8,128)}, u32[]{:S(2)}) copy-start(f32[3,32,128]{2,1,0:T(8,128)} %param.19) | copy-start | bytes 147460
  20.7 19.5 %collective-permute-start.4 = (f32[40,1,128]{0,2,1:T(8,128)S(1)}, f32[40,1,128]{0,2,1:T(8,128)S(1)}, u32[]{:S(2)}, u32[]{:S(2)}) collective-permute-start(f32[40,1,128]{0,2,1:T(8,128)S(1)} %get-tuple-element.434), channel_id=1, source_target_pairs={{2,0},{4,2},{6,4},{3,1},{5,3},{7,5},{10,8},{12,10},{14,12},{11,9},... | collective-permute-start | bytes 61448 | tf_op jit(solution)/shard_map/ppermute | solution.py:24
  22.0 18.2 %collective-permute-start.5 = (f32[40,1,128]{0,2,1:T(8,128)S(1)}, f32[40,1,128]{0,2,1:T(8,128)S(1)}, u32[]{:S(2)}, u32[]{:S(2)}) collective-permute-start(f32[40,1,128]{0,2,1:T(8,128)S(1)} %get-tuple-element.433), channel_id=1, source_target_pairs={{0,2},{2,4},{4,6},{1,3},{3,5},{5,7},{8,10},{10,12},{12,14},{9,11},... | collective-permute-start | bytes 61448 | tf_op jit(solution)/shard_map/ppermute | solution.py:22
  35.4 11.9 %collective-permute-start.8 = (f32[5,3,4,128]{3,2,1,0:T(4,128)S(1)}, f32[5,3,4,128]{3,2,1,0:T(4,128)S(1)}, u32[]{:S(2)}, u32[]{:S(2)}) collective-permute-start(f32[5,3,4,128]{3,2,1,0:T(4,128)S(1)} %get-tuple-element.457), channel_id=1, source_target_pairs={{0,2},{2,4},{4,6},{1,3},{3,5},{5,7},{8,10},{10,12},{12,14},{9,11},... | collective-permute-start | bytes 92168 | tf_op jit(solution)/shard_map/ppermute | solution.py:22
  39.0 8.4 %collective-permute-start.9 = (f32[5,3,4,128]{3,2,1,0:T(4,128)S(1)}, f32[5,3,4,128]{3,2,1,0:T(4,128)S(1)}, u32[]{:S(2)}, u32[]{:S(2)}) collective-permute-start(f32[5,3,4,128]{3,2,1,0:T(4,128)S(1)} %get-tuple-element.458), channel_id=1, source_target_pairs={{2,0},{4,2},{6,4},{3,1},{5,3},{7,5},{10,8},{12,10},{14,12},{11,9},... | collective-permute-start | bytes 92168 | tf_op jit(solution)/shard_map/ppermute | solution.py:24
  40.9 9.2 %collective-permute-start.6 = (f32[40,34,1]{0,2,1:T(1,128)}, f32[40,34,1]{0,2,1:T(1,128)S(1)}, u32[]{:S(2)}, u32[]{:S(2)}) collective-permute-start(f32[40,34,1]{0,2,1:T(1,128)} %get-tuple-element.432), channel_id=1, source_target_pairs={{1,0},{3,2},{5,4},{7,6},{9,8},{11,10},{13,12},{15,14},{17,16},{19,... | collective-permute-start | bytes 16328 | tf_op jit(solution)/shard_map/ppermute | solution.py:24
  42.2 7.9 %collective-permute-start.7 = (f32[40,34,1]{0,2,1:T(1,128)}, f32[40,34,1]{0,2,1:T(1,128)}, u32[]{:S(2)}, u32[]{:S(2)}) collective-permute-start(f32[40,34,1]{0,2,1:T(1,128)} %get-tuple-element.431), channel_id=1, source_target_pairs={{0,1},{2,3},{4,5},{6,7},{8,9},{10,11},{12,13},{14,15},{16,17},{18,... | collective-permute-start | bytes 16328 | tf_op jit(solution)/shard_map/ppermute | solution.py:22
  47.5 5.9 %collective-permute-start.10 = (f32[5,3,40,4]{3,2,1,0:T(8,128)S(1)}, f32[5,3,40,4]{3,2,1,0:T(8,128)S(1)}, u32[]{:S(2)}, u32[]{:S(2)}) collective-permute-start(f32[5,3,40,4]{3,2,1,0:T(8,128)S(1)} %get-tuple-element.453), channel_id=1, source_target_pairs={{0,1},{2,3},{4,5},{6,7},{8,9},{10,11},{12,13},{14,15},{16,17},{18,... | collective-permute-start | bytes 28808 | tf_op jit(solution)/shard_map/ppermute | solution.py:22
  48.8 4.6 %collective-permute-start.11 = (f32[5,3,40,4]{3,2,1,0:T(8,128)S(1)}, f32[5,3,40,4]{3,2,1,0:T(8,128)S(1)}, u32[]{:S(2)}, u32[]{:S(2)}) collective-permute-start(f32[5,3,40,4]{3,2,1,0:T(8,128)S(1)} %get-tuple-element.454), channel_id=1, source_target_pairs={{1,0},{3,2},{5,4},{7,6},{9,8},{11,10},{13,12},{15,14},{17,16},{19,... | collective-permute-start | bytes 28808 | tf_op jit(solution)/shard_map/ppermute | solution.py:24
  54.2 0.9 copy-start.3
  54.3 0.9 copy-start.7
  54.3 1.7 %copy-start = (f32[40,34,129]{0,2,1:T(8,128)S(1)}, f32[40,34,129]{0,2,1:T(8,128)}, u32[]{:S(2)}) copy-start(f32[40,34,129]{0,2,1:T(8,128)} %get-tuple-element.429) | copy-start | bytes 2105284
  62.6 1.1 %copy-start.1 = (f32[40,33,128]{2,1,0:T(8,128)S(1)}, f32[40,33,128]{2,1,0:T(8,128)}, u32[]{:S(2)}) copy-start(f32[40,33,128]{2,1,0:T(8,128)} %get-tuple-element.158) | copy-start | bytes 2027524 | tf_op jit(solution)/shard_map/cond
  62.6 1.4 %copy-start.2 = (f32[40,33,128]{2,1,0:T(8,128)S(1)}, f32[40,33,128]{2,1,0:T(8,128)}, u32[]{:S(2)}) copy-start(f32[40,33,128]{2,1,0:T(8,128)} %get-tuple-element.157) | copy-start | bytes 2027524 | tf_op jit(solution)/shard_map/cond
  75.7 6.1 %collective-permute-start.12 = (f32[5,3,4,128]{3,2,1,0:T(4,128)S(1)}, f32[5,3,4,128]{3,2,1,0:T(4,128)S(1)}, u32[]{:S(2)}, u32[]{:S(2)}) collective-permute-start(f32[5,3,4,128]{3,2,1,0:T(4,128)S(1)} %get-tuple-element.455), channel_id=1, source_target_pairs={{0,2},{2,4},{4,6},{1,3},{3,5},{5,7},{8,10},{10,12},{12,14},{9,11},... | collective-permute-start | bytes 92168 | tf_op jit(solution)/shard_map/ppermute | solution.py:22
  80.2 5.8 %collective-permute-start.13 = (f32[5,3,4,128]{3,2,1,0:T(4,128)S(1)}, f32[5,3,4,128]{3,2,1,0:T(4,128)S(1)}, u32[]{:S(2)}, u32[]{:S(2)}) collective-permute-start(f32[5,3,4,128]{3,2,1,0:T(4,128)S(1)} %get-tuple-element.456), channel_id=1, source_target_pairs={{2,0},{4,2},{6,4},{3,1},{5,3},{7,5},{10,8},{12,10},{14,12},{11,9},... | collective-permute-start | bytes 92168 | tf_op jit(solution)/shard_map/ppermute | solution.py:24
  86.2 2.6 %collective-permute-start.14 = (f32[5,3,40,4]{3,2,1,0:T(8,128)S(1)}, f32[5,3,40,4]{3,2,1,0:T(8,128)S(1)}, u32[]{:S(2)}, u32[]{:S(2)}) collective-permute-start(f32[5,3,40,4]{3,2,1,0:T(8,128)S(1)} %get-tuple-element.451), channel_id=1, source_target_pairs={{0,1},{2,3},{4,5},{6,7},{8,9},{10,11},{12,13},{14,15},{16,17},{18,... | collective-permute-start | bytes 28808 | tf_op jit(solution)/shard_map/ppermute | solution.py:22
  87.5 3.5 %collective-permute-start.15 = (f32[5,3,40,4]{3,2,1,0:T(8,128)S(1)}, f32[5,3,40,4]{3,2,1,0:T(8,128)S(1)}, u32[]{:S(2)}, u32[]{:S(2)}) collective-permute-start(f32[5,3,40,4]{3,2,1,0:T(8,128)S(1)} %get-tuple-element.452), channel_id=1, source_target_pairs={{1,0},{3,2},{5,4},{7,6},{9,8},{11,10},{13,12},{15,14},{17,16},{19,... | collective-permute-start | bytes 28808 | tf_op jit(solution)/shard_map/ppermute | solution.py:24
where the time goes:
time: 94.5 us; the launch traced here: 93.6 us
  starting transfers between devices  37.9 us (40%)
  other arithmetic  18.1 us (19%)
  blocking collectives  15.9 us (17%)
  local copies, waits for them, and re-layouts  13.9 us (15%)
  waiting for transfers between devices  6.69 us (7%)
    ppermute x8, starting transfers between devices, extended(): lax.ppermute(tail, axis, [(i, (i + 1) % count) for i in range(ends)])  27.5 us
    all_gather x2, blocking collectives, on_device(): basal_rows = lax.all_gather(velocity[:1], 'sec', axis=0, tiled=True)  15.9 us
    ppermute x8, starting transfers between devices, extended(): lax.ppermute(head, axis, [((i + 1) % count, i) for i in range(ends)])  10.3 us
    another operation x7, local copies, waits for them, and re-layouts  7.61 us
    concatenate x9, other arithmetic, extended(): jnp.concatenate([lax.ppermute(tail, axis, [(i, (i + 1) % count) for i in...  6.56 us
    ppermute x8, waiting for transfers between devices, extended(): lax.ppermute(head, axis, [((i + 1) % count, i) for i in range(ends)])  6.41 us
    add x2, other arithmetic, ice_core(): right_side = driving + viscous * (x_plus + x_minus + y_plus + y_minus)  4.17 us
    select_n x7, other arithmetic, sweep_padded(): jnp.where(inside > 0.5, numerator / (denominator + (1.0 - inside)), 0.0)  2.73 us
  transfers between devices with their start and end apart: 16, of which 3 were waited for; matrix products, arithmetic and copies ran while one was open for 10% of the time, Pallas kernels for 0%

commit v1 on v0

--- a/solution.py
+++ b/solution.py
@@ -9,6 +9,23 @@
 VERT = 4.0
 FLOOR = 0.25
 HEATING = 0.5
+
+
+def joined_along(pieces, dim):
+    lengths = list(pieces.shape[1:])
+    lengths[dim] *= pieces.shape[0]
+    return jnp.moveaxis(pieces, 0, dim).reshape(lengths)
+
+
+def gather_around(x, axis, dim):
+    count = lax.axis_size(axis)
+    upward = [(i, (i + 1) % count) for i in range(count)]
+    tiles = [x]
+    while len(tiles) < count:
+        tiles.append(lax.ppermute(tiles[-1], axis, upward))
+    index = lax.axis_index(axis)
+    tiles = jnp.stack(tiles)[(index - jnp.arange(count)) % count]
+    return joined_along(tiles, dim)
 
 
 def extended(cells, sides, width):
@@ -143,7 +160,7 @@
             ),
             lambda: jnp.zeros_like(old_velocity),
         )
-        basal_rows = lax.all_gather(velocity[:1], "sec", axis=0, tiled=True)
+        basal_rows = gather_around(velocity[:1], "sec", 0)
         sliding = basal_rows[:sectors]
         squared = sliding * sliding
         trans_eff = transmissivity * (1.0 + squared / (1.0 + squared))

time: 94.5 us -> 108 us (1.14)
  waiting for transfers between devices: 6.69 us -> 26.8 us
  blocking collectives: 15.9 us -> 0 us
  starting transfers between devices: 37.9 us -> 42.3 us
  local copies, waits for them, and re-layouts: 13.9 us -> 17.1 us
  other arithmetic: 18.1 us -> 19.6 us
    ppermute x0 -> x6, waiting for transfers between devices: none -> 16.4 us  [gather_around(): tiles.append(lax.ppermute(tiles[-1], axis, upward))]
    all_gather x2 -> x0, blocking collectives: 15.9 us -> none  [on_device(): basal_rows = lax.all_gather(velocity[:1], 'sec', axis=0, tiled=True)]
    ppermute x0 -> x6, starting transfers between devices: none -> 4.98 us  [gather_around(): tiles.append(lax.ppermute(tiles[-1], axis, upward))]
    ppermute x8, waiting for transfers between devices: 6.41 us -> 9.58 us  [extended(): lax.ppermute(head, axis, [((i + 1) % count, i) for i in range(ends)])]
    gather x0 -> x2, local copies, waits for them, and re-layouts: none -> 1.22 us  [gather_around(): tiles = jnp.stack(tiles)[(index - jnp.arange(count)) % count]]
    cond x42 -> x43, local copies, waits for them, and re-layouts: 1.47 us -> 2.19 us
    another operation x7 -> x8, local copies, waits for them, and re-layouts: 7.61 us -> 8.23 us
  transfers between devices with their start and end apart: 16 -> 22, of which waited for: 3 -> 9; matrix products, arithmetic and copies ran while one was open for 10% -> 10% of each run, Pallas kernels for 0% -> 0%
where the time goes in v1:
time: 108 us; the launch traced here: 107 us
  starting transfers between devices  42.3 us (39%)
  waiting for transfers between devices  26.8 us (25%)
  other arithmetic  19.6 us (18%)
  local copies, waits for them, and re-layouts  17.1 us (16%)
    ppermute x8, starting transfers between devices, extended(): lax.ppermute(tail, axis, [(i, (i + 1) % count) for i in range(ends)])  27 us
    ppermute x6, waiting for transfers between devices, gather_around(): tiles.append(lax.ppermute(tiles[-1], axis, upward))  16.4 us
    ppermute x8, starting transfers between devices, extended(): lax.ppermute(head, axis, [((i + 1) % count, i) for i in range(ends)])  10.3 us
    ppermute x8, waiting for transfers between devices, extended(): lax.ppermute(head, axis, [((i + 1) % count, i) for i in range(ends)])  9.58 us
    another operation x7, local copies, waits for them, and re-layouts  7.63 us
    concatenate x9, other arithmetic, extended(): jnp.concatenate([lax.ppermute(tail, axis, [(i, (i + 1) % count) for i in...  6.56 us
    ppermute x6, starting transfers between devices, gather_around(): tiles.append(lax.ppermute(tiles[-1], axis, upward))  4.98 us
    add x2, other arithmetic, ice_core(): right_side = driving + viscous * (x_plus + x_minus + y_plus + y_minus)  4.17 us
  transfers between devices with their start and end apart: 22, of which 9 were waited for; matrix products, arithmetic and copies ran while one was open for 10% of the time, Pallas kernels for 0%

profile of v1, /device:TPU:0, one launch (start us, length us, event | category | flops | bytes accessed | tf_op | source)
XLA Modules:
  0.0 107.0 jit_solution(3042547285374319777)
XLA Ops:
  0.0 1.3 %collective-permute-start = (f32[40,1,128]{2,0,1:T(8,128)S(1)}, f32[40,1,128]{2,0,1:T(8,128)S(1)}, u32[]{:S(2)}, u32[]{:S(2)}) collective-permute-start(f32[40,1,128]{2,0,1:T(8,128)S(1)} %broadcast.6575), channel_id=1, source_target_pairs={{2,0},{4,2},{6,4},{3,1},{5,3},{7,5},{10,8},{12,10},{14,12},{11,9},... | collective-permute-start | bytes 61448 | tf_op jit(solution)/shard_map/ppermute | solution.py:41
  1.3 5.6 %collective-permute-start.1 = (f32[40,1,128]{2,0,1:T(8,128)S(1)}, f32[40,1,128]{2,0,1:T(8,128)S(1)}, u32[]{:S(2)}, u32[]{:S(2)}) collective-permute-start(f32[40,1,128]{2,0,1:T(8,128)S(1)} %broadcast.6575), channel_id=1, source_target_pairs={{0,2},{2,4},{4,6},{1,3},{3,5},{5,7},{8,10},{10,12},{12,14},{9,11},... | collective-permute-start | bytes 61448 | tf_op jit(solution)/shard_map/ppermute | solution.py:39
  6.9 0.8 bitcast_dynamic-update-slice_fusion.5
  7.7 0.8 convert_multiply_fusion
  8.5 0.7 dynamic-slice_bitcast_fusion
  9.3 0.7 convert_bitcast_fusion
  10.6 1.3 %collective-permute-start.2 = (f32[40,34,1]{0,2,1:T(1,128)S(1)}, f32[40,34,1]{0,2,1:T(1,128)S(1)}, u32[]{:S(2)}, u32[]{:S(2)}) collective-permute-start(f32[40,34,1]{0,2,1:T(1,128)S(1)} %copy.56), channel_id=1, source_target_pairs={{1,0},{3,2},{5,4},{7,6},{9,8},{11,10},{13,12},{15,14},{17,16},{19,... | collective-permute-start | bytes 16328 | tf_op jit(solution)/shard_map/ppermute | solution.py:41
  12.2 3.0 %collective-permute-start.3 = (f32[40,34,1]{0,2,1:T(1,128)S(1)}, f32[40,34,1]{0,2,1:T(1,128)S(1)}, u32[]{:S(2)}, u32[]{:S(2)}) collective-permute-start(f32[40,34,1]{0,2,1:T(1,128)S(1)} %copy.57), channel_id=1, source_target_pairs={{0,1},{2,3},{4,5},{6,7},{8,9},{10,11},{12,13},{14,15},{16,17},{18,... | collective-permute-start | bytes 16328 | tf_op jit(solution)/shard_map/ppermute | solution.py:39
  16.9 3.6 %conditional.2 = (f32[40,32,128]{2,1,0:T(8,128)S(1)}) conditional(s32[]{:T(128)} %convert_element_type.13, () %tuple.32, (f32[32,128]{1,0:T(8,128)S(1)}, f32[32,128]{1,0:T(8,128)S(1)}, f32[40,1,128]{2,0,1:T(8,128)S(1)}, f32[40,1,128]{2,0,1:T(8,128)S(1)}, f32[40,34,129]{2,0,1:T(8,128)S(1)}, /*index=5*/f32[40,34,129]{2,0,1:T(8,128)S(1)}, ...), branch_computations={%region_0.1_spmd, %region_1.2_spmd} | conditional | flops 5099559 | bytes 16611208 | solution.py:148
  17.8 1.2 %multiply_add_fusion = (f32[40,32,128]{2,1,0:T(8,128)S(1)}, f32[40,32,128]{2,1,0:T(8,128)S(1)}) fusion(f32[40,34,129]{2,1,0:T(8,128)S(1)} %copy.48, f32[40,34,129]{2,1,0:T(8,128)S(1)} %copy.47, f32[40,1,128]{2,1,0:T(1,128)S(1)} %bitcast.64, f32[40,1,128]{2,1,0:T(1,128)S(1)} %bitcast.65, f32[32,128]{1,0:T(8,128)S(1)} %get-tuple-element.148, ...), kind=kLoop, calls=%fused_computation.4 | loop fusion | flops 2457600 | bytes 2695328 | tf_op jit(solution)/shard_map/cond/branch_1_fun/add | solution.py:59
  20.5 0.6 copy.49
  21.2 0.6 slice_bitcast_fusion.10
  21.8 1.9 %collective-permute-start.8 = (f32[1,32,128]{2,1,0:T(8,128)S(1)}, f32[1,32,128]{2,1,0:T(8,128)S(1)}, u32[]{:S(2)}, u32[]{:S(2)}) collective-permute-start(f32[1,32,128]{2,1,0:T(8,128)S(1)} %get-tuple-element.447), channel_id=1, source_target_pairs={{0,8},{8,16},{16,24},{24,0},{1,9},{9,17},{17,25},{25,1},{2,10},{10... | collective-permute-start | bytes 49160 | tf_op jit(solution)/shard_map/ppermute | solution.py:25
  23.7 1.3 %collective-permute-start.4 = (f32[40,1,128]{0,2,1:T(8,128)S(1)}, f32[40,1,128]{0,2,1:T(8,128)S(1)}, u32[]{:S(2)}, u32[]{:S(2)}) collective-permute-start(f32[40,1,128]{0,2,1:T(8,128)S(1)} %get-tuple-element.439), channel_id=1, source_target_pairs={{2,0},{4,2},{6,4},{3,1},{5,3},{7,5},{10,8},{12,10},{14,12},{11,9},... | collective-permute-start | bytes 61448 | tf_op jit(solution)/shard_map/ppermute | solution.py:41
  25.0 4.5 %collective-permute-start.5 = (f32[40,1,128]{0,2,1:T(8,128)S(1)}, f32[40,1,128]{0,2,1:T(8,128)S(1)}, u32[]{:S(2)}, u32[]{:S(2)}) collective-permute-start(f32[40,1,128]{0,2,1:T(8,128)S(1)} %get-tuple-element.438), channel_id=1, source_target_pairs={{0,2},{2,4},{4,6},{1,3},{3,5},{5,7},{8,10},{10,12},{12,14},{9,11},... | collective-permute-start | bytes 61448 | tf_op jit(solution)/shard_map/ppermute | solution.py:39
  29.6 1.5 %collective-permute-start.9 = (f32[1,32,128]{2,1,0:T(8,128)S(1)}, f32[1,32,128]{2,1,0:T(8,128)}, u32[]{:S(2)}, u32[]{:S(2)}) collective-permute-start(f32[1,32,128]{2,1,0:T(8,128)S(1)} %collective-permute-done.8), channel_id=1, source_target_pairs={{0,8},{8,16},{16,24},{24,0},{1,9},{9,17},{17,25},{25,1},{2,10},{10... | collective-permute-start | bytes 49160 | tf_op jit(solution)/shard_map/ppermute | solution.py:25
  31.2 3.2 %collective-permute-done.9 = f32[1,32,128]{2,1,0:T(8,128)} collective-permute-done((f32[1,32,128]{2,1,0:T(8,128)S(1)}, f32[1,32,128]{2,1,0:T(8,128)}, u32[]{:S(2)}, u32[]{:S(2)}) %collective-permute-start.9) | collective-permute-done | bytes 16416 | tf_op jit(solution)/shard_map/ppermute | solution.py:25
  34.4 0.6 collective-permute-start.10
  35.0 0.6 pad_maximum_fusion.9
  35.7 1.3 %collective-permute-start.6 = (f32[40,34,1]{0,2,1:T(1,128)}, f32[40,34,1]{0,2,1:T(1,128)}, u32[]{:S(2)}, u32[]{:S(2)}) collective-permute-start(f32[40,34,1]{0,2,1:T(1,128)} %get-tuple-element.437), channel_id=1, source_target_pairs={{1,0},{3,2},{5,4},{7,6},{9,8},{11,10},{13,12},{15,14},{17,16},{19,... | collective-permute-start | bytes 16328 | tf_op jit(solution)/shard_map/ppermute | solution.py:41
  37.0 4.2 %collective-permute-start.7 = (f32[40,34,1]{0,2,1:T(1,128)}, f32[40,34,1]{0,2,1:T(1,128)}, u32[]{:S(2)}, u32[]{:S(2)}) collective-permute-start(f32[40,34,1]{0,2,1:T(1,128)} %get-tuple-element.436), channel_id=1, source_target_pairs={{0,1},{2,3},{4,5},{6,7},{8,9},{10,11},{12,13},{14,15},{16,17},{18,... | collective-permute-start | bytes 16328 | tf_op jit(solution)/shard_map/ppermute | solution.py:39
  41.3 0.8 maximum_bitcast_fusion
  42.8 3.5 %collective-permute-start.11 = (f32[5,3,4,128]{3,2,1,0:T(4,128)S(1)}, f32[5,3,4,128]{3,2,1,0:T(4,128)S(1)}, u32[]{:S(2)}, u32[]{:S(2)}) collective-permute-start(f32[5,3,4,128]{3,2,1,0:T(4,128)S(1)} %get-tuple-element.464), channel_id=1, source_target_pairs={{0,2},{2,4},{4,6},{1,3},{3,5},{5,7},{8,10},{10,12},{12,14},{9,11},... | collective-permute-start | bytes 92168 | tf_op jit(solution)/shard_map/ppermute | solution.py:39
  46.3 1.3 %collective-permute-start.12 = (f32[5,3,4,128]{3,2,1,0:T(4,128)S(1)}, f32[5,3,4,128]{3,2,1,0:T(4,128)S(1)}, u32[]{:S(2)}, u32[]{:S(2)}) collective-permute-start(f32[5,3,4,128]{3,2,1,0:T(4,128)S(1)} %get-tuple-element.465), channel_id=1, source_target_pairs={{2,0},{4,2},{6,4},{3,1},{5,3},{7,5},{10,8},{12,10},{14,12},{11,9},... | collective-permute-start | bytes 92168 | tf_op jit(solution)/shard_map/ppermute | solution.py:41
  47.6 1.3 %pad_maximum_fusion.3 = (f32[40,33,128]{2,1,0:T(8,128)}, f32[40,33,128]{2,1,0:T(8,128)}) fusion(f32[40,32,128]{2,1,0:T(8,128)S(1)} %get-tuple-element.474, f32[40,1,128]{2,1,0:T(1,128)S(1)} %copy.52, f32[40,1,128]{2,1,0:T(1,128)S(1)} %copy.50), kind=kLoop, calls=%fused_computation.729 | loop fusion | flops 337920 | bytes 2048000 | tf_op jit(solution)/shard_map/concatenate | solution.py:37
  48.9 3.2 %collective-permute-done.12 = f32[5,3,4,128]{3,2,1,0:T(4,128)S(1)} collective-permute-done((f32[5,3,4,128]{3,2,1,0:T(4,128)S(1)}, f32[5,3,4,128]{3,2,1,0:T(4,128)S(1)}, u32[]{:S(2)}, u32[]{:S(2)}) %collective-permute-start.12) | collective-permute-done | bytes 30752 | tf_op jit(solution)/shard_map/ppermute | solution.py:41
  52.3 1.3 %collective-permute-start.13 = (f32[5,3,40,4]{3,2,1,0:T(8,128)S(1)}, f32[5,3,40,4]{3,2,1,0:T(8,128)S(1)}, u32[]{:S(2)}, u32[]{:S(2)}) collective-permute-start(f32[5,3,40,4]{3,2,1,0:T(8,128)S(1)} %get-tuple-element.460), channel_id=1, source_target_pairs={{0,1},{2,3},{4,5},{6,7},{8,9},{10,11},{12,13},{14,15},{16,17},{18,... | collective-permute-start | bytes 28808 | tf_op jit(solution)/shard_map/ppermute | solution.py:39
  53.6 1.3 %collective-permute-start.14 = (f32[5,3,40,4]{3,2,1,0:T(8,128)S(1)}, f32[5,3,40,4]{3,2,1,0:T(8,128)S(1)}, u32[]{:S(2)}, u32[]{:S(2)}) collective-permute-start(f32[5,3,40,4]{3,2,1,0:T(8,128)S(1)} %get-tuple-element.461), channel_id=1, source_target_pairs={{1,0},{3,2},{5,4},{7,6},{9,8},{11,10},{13,12},{15,14},{17,16},{19,... | collective-permute-start | bytes 28808 | tf_op jit(solution)/shard_map/ppermute | solution.py:41
  54.9 3.3 %maximum_maximum_fusion = (f32[40,34,129]{0,2,1:T(8,128)}, f32[40,34,129]{0,2,1:T(8,128)}) fusion(f32[40,1,128]{0,2,1:T(8,128)S(1)} %collective-permute-done.4, f32[40,32,128]{0,2,1:T(8,128)S(1)} %copy.49, f32[40,1,128]{0,2,1:T(8,128)S(1)} %collective-permute-done.5, f32[40,34,1]{0,2,1:T(1,128)} %collective-permute-done.7, ...), kind=kLoop, calls=%fused_computation.725 | loop fusion | flops 1052640 | bytes 2110720 | tf_op jit(solution)/shard_map/concatenate | solution.py:37
  60.8 13.7 %conditional.3 = (f32[1,32,128]{2,1,0:T(8,128)S(1)}, f32[1,32,128]{2,1,0:T(8,128)}, f32[1,1,32,128]{3,2,1,0:T(8,128)S(1)}) conditional(s32[]{:T(128)} %convert_element_type.13, () %tuple.31, (f32[32,128]{1,0:T(8,128)S(1)}, f32[32,128]{1,0:T(8,128)S(1)}, f32[40,32,128]{2,1,0:T(8,128)S(1)}, f32[40,33,128]{2,1,0:T(8,128)}, f32[40,33,128]{2,1,0:T(8,128)}, ...), branch_computations={%region_2.3_spmd, %region_3.4_spmd} | conditional | flops 5423103 | bytes 25941332 | solution.py:148
  60.8 4.1 %copy.54 = f32[40,34,129]{2,1,0:T(8,128)} copy(f32[40,34,129]{0,2,1:T(8,128)} %get-tuple-element.225) | data formatting | bytes 1403520 | tf_op jit(solution)/shard_map
  64.8 2.6 %copy.55 = f32[40,34,129]{2,1,0:T(8,128)} copy(f32[40,34,129]{0,2,1:T(8,128)S(1)} %get-tuple-element.226) | data formatting | bytes 1403520 | tf_op jit(solution)/shard_map
  67.5 1.1 %copy-done.1 = f32[40,33,128]{2,1,0:T(8,128)S(1)} copy-done((f32[40,33,128]{2,1,0:T(8,128)S(1)}, f32[40,33,128]{2,1,0:T(8,128)}, u32[]{:S(2)}) %copy-start.1) | copy-done | bytes 675864 | tf_op jit(solution)/shard_map/cond
  68.8 2.9 %multiply_add_fusion.39 = (f32[40,32,128]{2,1,0:T(8,128)S(1)}, f32[40,32,128]{2,1,0:T(8,128)S(1)}) fusion(f32[40,34,129]{2,1,0:T(8,128)} %copy.55, f32[40,34,129]{2,1,0:T(8,128)} %copy.54, f32[40,33,128]{2,1,0:T(8,128)S(1)} %copy-done.1, f32[40,33,128]{2,1,0:T(8,128)S(1)} %copy-done.2, f32[32,128]{1,0:T(8,128)S(1)} %get-tuple-element.157, ...), kind=kLoop, calls=%fused_computation.364 | loop fusion | flops 2621440 | bytes 4603904 | tf_op jit(solution)/shard_map/cond/branch_1_fun/add | solution.py:59
  73.2 0.6 fusion.590
  73.8 0.7 copy.147
  74.5 0.9 collective-permute-start.15
  75.4 3.9 %collective-permute-done.15 = f32[1,32,128]{2,1,0:T(8,128)S(1)} collective-permute-done((f32[1,32,128]{2,1,0:T(8,128)}, f32[1,32,128]{2,1,0:T(8,128)S(1)}, u32[]{:S(2)}, u32[]{:S(2)}) %collective-permute-start.15) | collective-permute-done | bytes 16416 | tf_op jit(solution)/shard_map/ppermute | solution.py:25
  79.4 4.6 %collective-permute-done.16 = f32[1,32,128]{2,1,0:T(8,128)S(1)} collective-permute-done((f32[1,32,128]{2,1,0:T(8,128)S(1)}, f32[1,32,128]{2,1,0:T(8,128)S(1)}, u32[]{:S(2)}, u32[]{:S(2)}) %collective-permute-start.16) | collective-permute-done | bytes 16416 | tf_op jit(solution)/shard_map/ppermute | solution.py:25
  84.0 4.6 %collective-permute-done.17 = f32[1,32,128]{2,1,0:T(8,128)S(1)} collective-permute-done((f32[1,32,128]{2,1,0:T(8,128)S(1)}, f32[1,32,128]{2,1,0:T(8,128)S(1)}, u32[]{:S(2)}, u32[]{:S(2)}) %collective-permute-start.17) | collective-permute-done | bytes 16416 | tf_op jit(solution)/shard_map/ppermute | solution.py:25
  88.6 0.7 gather_fusion.1
  89.4 3.5 %collective-permute-start.18 = (f32[5,3,4,128]{3,2,1,0:T(4,128)S(1)}, f32[5,3,4,128]{3,2,1,0:T(4,128)S(1)}, u32[]{:S(2)}, u32[]{:S(2)}) collective-permute-start(f32[5,3,4,128]{3,2,1,0:T(4,128)S(1)} %get-tuple-element.462), channel_id=1, source_target_pairs={{0,2},{2,4},{4,6},{1,3},{3,5},{5,7},{8,10},{10,12},{12,14},{9,11},... | collective-permute-start | bytes 92168 | tf_op jit(solution)/shard_map/ppermute | solution.py:39
  92.9 1.3 %collective-permute-start.19 = (f32[5,3,4,128]{3,2,1,0:T(4,128)S(1)}, f32[5,3,4,128]{3,2,1,0:T(4,128)S(1)}, u32[]{:S(2)}, u32[]{:S(2)}) collective-permute-start(f32[5,3,4,128]{3,2,1,0:T(4,128)S(1)} %get-tuple-element.463), channel_id=1, source_target_pairs={{2,0},{4,2},{6,4},{3,1},{5,3},{7,5},{10,8},{12,10},{14,12},{11,9},... | collective-permute-start | bytes 92168 | tf_op jit(solution)/shard_map/ppermute | solution.py:41
  94.5 4.2 %collective-permute-done.19 = f32[5,3,4,128]{3,2,1,0:T(4,128)S(1)} collective-permute-done((f32[5,3,4,128]{3,2,1,0:T(4,128)S(1)}, f32[5,3,4,128]{3,2,1,0:T(4,128)S(1)}, u32[]{:S(2)}, u32[]{:S(2)}) %collective-permute-start.19) | collective-permute-done | bytes 30752 | tf_op jit(solution)/shard_map/ppermute | solution.py:41
  98.9 1.3 %collective-permute-start.20 = (f32[5,3,40,4]{3,2,1,0:T(8,128)S(1)}, f32[5,3,40,4]{3,2,1,0:T(8,128)S(1)}, u32[]{:S(2)}, u32[]{:S(2)}) collective-permute-start(f32[5,3,40,4]{3,2,1,0:T(8,128)S(1)} %get-tuple-element.458), channel_id=1, source_target_pairs={{0,1},{2,3},{4,5},{6,7},{8,9},{10,11},{12,13},{14,15},{16,17},{18,... | collective-permute-start | bytes 28808 | tf_op jit(solution)/shard_map/ppermute | solution.py:39
  100.2 1.3 %collective-permute-start.21 = (f32[5,3,40,4]{3,2,1,0:T(8,128)S(1)}, f32[5,3,40,4]{3,2,1,0:T(8,128)S(1)}, u32[]{:S(2)}, u32[]{:S(2)}) collective-permute-start(f32[5,3,40,4]{3,2,1,0:T(8,128)S(1)} %get-tuple-element.459), channel_id=1, source_target_pairs={{1,0},{3,2},{5,4},{7,6},{9,8},{11,10},{13,12},{15,14},{17,16},{19,... | collective-permute-start | bytes 28808 | tf_op jit(solution)/shard_map/ppermute | solution.py:41
  101.5 2.2 %collective-permute-done.21 = f32[5,3,40,4]{3,2,1,0:T(8,128)S(1)} collective-permute-done((f32[5,3,40,4]{3,2,1,0:T(8,128)S(1)}, f32[5,3,40,4]{3,2,1,0:T(8,128)S(1)}, u32[]{:S(2)}, u32[]{:S(2)}) %collective-permute-start.21) | collective-permute-done | bytes 9632 | tf_op jit(solution)/shard_map/ppermute | solution.py:41
  105.6 1.3 %fusion.436 = f32[1,3,32,128]{3,2,1,0:T(8,128)} fusion(f32[3,32,128]{2,1,0:T(8,128)S(1)} %fusion.413, f32[1,32,128]{2,1,0:T(8,128)S(1)} %dynamic-slice_multiply_fusion, f32[1,32,128]{2,1,0:T(8,128)} %get-tuple-element.171, f32[1,32,128]{2,1,0:T(8,128)S(1)} %get-tuple-element.170, pred[]{:T(512)S(6)} %lt.32), kind=kLoop, calls=%fused_computation.944 | loop fusion | flops 36864 | bytes 147457 | tf_op jit(solution)/shard_map/broadcast_in_dim | solution.py:173
  (178 shorter events, 11.9 us)
Async XLA Ops:
  0.0 10.0 %collective-permute-start = (f32[40,1,128]{2,0,1:T(8,128)S(1)}, f32[40,1,128]{2,0,1:T(8,128)S(1)}, u32[]{:S(2)}, u32[]{:S(2)}) collective-permute-start(f32[40,1,128]{2,0,1:T(8,128)S(1)} %broadcast.6575), channel_id=1, source_target_pairs={{2,0},{4,2},{6,4},{3,1},{5,3},{7,5},{10,8},{12,10},{14,12},{11,9},... | collective-permute-start | bytes 61448 | tf_op jit(solution)/shard_map/ppermute | solution.py:41
  1.3 8.7 %collective-permute-start.1 = (f32[40,1,128]{2,0,1:T(8,128)S(1)}, f32[40,1,128]{2,0,1:T(8,128)S(1)}, u32[]{:S(2)}, u32[]{:S(2)}) collective-permute-start(f32[40,1,128]{2,0,1:T(8,128)S(1)} %broadcast.6575), channel_id=1, source_target_pairs={{0,2},{2,4},{4,6},{1,3},{3,5},{5,7},{8,10},{10,12},{12,14},{9,11},... | collective-permute-start | bytes 61448 | tf_op jit(solution)/shard_map/ppermute | solution.py:39
  10.6 4.7 %collective-permute-start.2 = (f32[40,34,1]{0,2,1:T(1,128)S(1)}, f32[40,34,1]{0,2,1:T(1,128)S(1)}, u32[]{:S(2)}, u32[]{:S(2)}) collective-permute-start(f32[40,34,1]{0,2,1:T(1,128)S(1)} %copy.56), channel_id=1, source_target_pairs={{1,0},{3,2},{5,4},{7,6},{9,8},{11,10},{13,12},{15,14},{17,16},{19,... | collective-permute-start | bytes 16328 | tf_op jit(solution)/shard_map/ppermute | solution.py:41
  12.2 3.9 %collective-permute-start.3 = (f32[40,34,1]{0,2,1:T(1,128)S(1)}, f32[40,34,1]{0,2,1:T(1,128)S(1)}, u32[]{:S(2)}, u32[]{:S(2)}) collective-permute-start(f32[40,34,1]{0,2,1:T(1,128)S(1)} %copy.57), channel_id=1, source_target_pairs={{0,1},{2,3},{4,5},{6,7},{8,9},{10,11},{12,13},{14,15},{16,17},{18,... | collective-permute-start | bytes 16328 | tf_op jit(solution)/shard_map/ppermute | solution.py:39
  21.2 21.5 %copy-start.5 = (f32[3,32,128]{2,1,0:T(8,128)S(1)}, f32[3,32,128]{2,1,0:T(8,128)}, u32[]{:S(2)}) copy-start(f32[3,32,128]{2,1,0:T(8,128)} %param.20) | copy-start | bytes 147460
  21.2 21.5 %copy-start.4 = (f32[3,32,128]{2,1,0:T(8,128)S(1)}, f32[3,32,128]{2,1,0:T(8,128)}, u32[]{:S(2)}) copy-start(f32[3,32,128]{2,1,0:T(8,128)} %param.21) | copy-start | bytes 147460
  21.2 21.5 %copy-start.6 = (f32[3,32,128]{2,1,0:T(8,128)S(1)}, f32[3,32,128]{2,1,0:T(8,128)}, u32[]{:S(2)}) copy-start(f32[3,32,128]{2,1,0:T(8,128)} %param.19) | copy-start | bytes 147460
  21.8 7.8 %collective-permute-start.8 = (f32[1,32,128]{2,1,0:T(8,128)S(1)}, f32[1,32,128]{2,1,0:T(8,128)S(1)}, u32[]{:S(2)}, u32[]{:S(2)}) collective-permute-start(f32[1,32,128]{2,1,0:T(8,128)S(1)} %get-tuple-element.447), channel_id=1, source_target_pairs={{0,8},{8,16},{16,24},{24,0},{1,9},{9,17},{17,25},{25,1},{2,10},{10... | collective-permute-start | bytes 49160 | tf_op jit(solution)/shard_map/ppermute | solution.py:25
  23.7 11.3 %collective-permute-start.4 = (f32[40,1,128]{0,2,1:T(8,128)S(1)}, f32[40,1,128]{0,2,1:T(8,128)S(1)}, u32[]{:S(2)}, u32[]{:S(2)}) collective-permute-start(f32[40,1,128]{0,2,1:T(8,128)S(1)} %get-tuple-element.439), channel_id=1, source_target_pairs={{2,0},{4,2},{6,4},{3,1},{5,3},{7,5},{10,8},{12,10},{14,12},{11,9},... | collective-permute-start | bytes 61448 | tf_op jit(solution)/shard_map/ppermute | solution.py:41
  25.0 10.0 %collective-permute-start.5 = (f32[40,1,128]{0,2,1:T(8,128)S(1)}, f32[40,1,128]{0,2,1:T(8,128)S(1)}, u32[]{:S(2)}, u32[]{:S(2)}) collective-permute-start(f32[40,1,128]{0,2,1:T(8,128)S(1)} %get-tuple-element.438), channel_id=1, source_target_pairs={{0,2},{2,4},{4,6},{1,3},{3,5},{5,7},{8,10},{10,12},{12,14},{9,11},... | collective-permute-start | bytes 61448 | tf_op jit(solution)/shard_map/ppermute | solution.py:39
  29.6 7.3 %copy-start.9 = (f32[1,32,128]{2,1,0:T(8,128)}, f32[1,32,128]{2,1,0:T(8,128)S(1)}, u32[]{:S(2)}) copy-start(f32[1,32,128]{2,1,0:T(8,128)S(1)} %collective-permute-done.8) | copy-start | bytes 49156
  29.6 4.8 %collective-permute-start.9 = (f32[1,32,128]{2,1,0:T(8,128)S(1)}, f32[1,32,128]{2,1,0:T(8,128)}, u32[]{:S(2)}, u32[]{:S(2)}) collective-permute-start(f32[1,32,128]{2,1,0:T(8,128)S(1)} %collective-permute-done.8), channel_id=1, source_target_pairs={{0,8},{8,16},{16,24},{24,0},{1,9},{9,17},{17,25},{25,1},{2,10},{10... | collective-permute-start | bytes 49160 | tf_op jit(solution)/shard_map/ppermute | solution.py:25
  31.2 11.6 %copy-start.10 = (s32[1024]{0:T(1024)}, s32[1024]{0:T(1024)S(1)}, u32[]{:S(2)}) copy-start(s32[1024]{0:T(1024)S(1)} %pad_clamp_fusion) | copy-start | bytes 12292
  34.4 6.9 %collective-permute-start.10 = (f32[1,32,128]{2,1,0:T(8,128)}, f32[1,32,128]{2,1,0:T(8,128)}, u32[]{:S(2)}, u32[]{:S(2)}) collective-permute-start(f32[1,32,128]{2,1,0:T(8,128)} %collective-permute-done.9), channel_id=1, source_target_pairs={{0,8},{8,16},{16,24},{24,0},{1,9},{9,17},{17,25},{25,1},{2,10},{10... | collective-permute-start | bytes 49160 | tf_op jit(solution)/shard_map/ppermute | solution.py:25
  35.0 6.3 %copy-start.8 = (f32[1,1,32,128]{3,2,1,0:T(8,128)S(1)}, f32[1,1,32,128]{3,2,1,0:T(8,128)}, u32[]{:S(2)}) copy-start(f32[1,1,32,128]{3,2,1,0:T(8,128)} %get-tuple-element.446) | copy-start | bytes 49156
  35.7 19.2 %collective-permute-start.6 = (f32[40,34,1]{0,2,1:T(1,128)}, f32[40,34,1]{0,2,1:T(1,128)}, u32[]{:S(2)}, u32[]{:S(2)}) collective-permute-start(f32[40,34,1]{0,2,1:T(1,128)} %get-tuple-element.437), channel_id=1, source_target_pairs={{1,0},{3,2},{5,4},{7,6},{9,8},{11,10},{13,12},{15,14},{17,16},{19,... | collective-permute-start | bytes 16328 | tf_op jit(solution)/shard_map/ppermute | solution.py:41
  37.0 17.9 %collective-permute-start.7 = (f32[40,34,1]{0,2,1:T(1,128)}, f32[40,34,1]{0,2,1:T(1,128)}, u32[]{:S(2)}, u32[]{:S(2)}) collective-permute-start(f32[40,34,1]{0,2,1:T(1,128)} %get-tuple-element.436), channel_id=1, source_target_pairs={{0,1},{2,3},{4,5},{6,7},{8,9},{10,11},{12,13},{14,15},{16,17},{18,... | collective-permute-start | bytes 16328 | tf_op jit(solution)/shard_map/ppermute | solution.py:39
  42.8 6.1 %collective-permute-start.11 = (f32[5,3,4,128]{3,2,1,0:T(4,128)S(1)}, f32[5,3,4,128]{3,2,1,0:T(4,128)S(1)}, u32[]{:S(2)}, u32[]{:S(2)}) collective-permute-start(f32[5,3,4,128]{3,2,1,0:T(4,128)S(1)} %get-tuple-element.464), channel_id=1, source_target_pairs={{0,2},{2,4},{4,6},{1,3},{3,5},{5,7},{8,10},{10,12},{12,14},{9,11},... | collective-permute-start | bytes 92168 | tf_op jit(solution)/shard_map/ppermute | solution.py:39
  46.3 5.8 %collective-permute-start.12 = (f32[5,3,4,128]{3,2,1,0:T(4,128)S(1)}, f32[5,3,4,128]{3,2,1,0:T(4,128)S(1)}, u32[]{:S(2)}, u32[]{:S(2)}) collective-permute-start(f32[5,3,4,128]{3,2,1,0:T(4,128)S(1)} %get-tuple-element.465), channel_id=1, source_target_pairs={{2,0},{4,2},{6,4},{3,1},{5,3},{7,5},{10,8},{12,10},{14,12},{11,9},... | collective-permute-start | bytes 92168 | tf_op jit(solution)/shard_map/ppermute | solution.py:41
  52.3 5.9 %collective-permute-start.13 = (f32[5,3,40,4]{3,2,1,0:T(8,128)S(1)}, f32[5,3,40,4]{3,2,1,0:T(8,128)S(1)}, u32[]{:S(2)}, u32[]{:S(2)}) collective-permute-start(f32[5,3,40,4]{3,2,1,0:T(8,128)S(1)} %get-tuple-element.460), channel_id=1, source_target_pairs={{0,1},{2,3},{4,5},{6,7},{8,9},{10,11},{12,13},{14,15},{16,17},{18,... | collective-permute-start | bytes 28808 | tf_op jit(solution)/shard_map/ppermute | solution.py:39
  53.6 4.6 %collective-permute-start.14 = (f32[5,3,40,4]{3,2,1,0:T(8,128)S(1)}, f32[5,3,40,4]{3,2,1,0:T(8,128)S(1)}, u32[]{:S(2)}, u32[]{:S(2)}) collective-permute-start(f32[5,3,40,4]{3,2,1,0:T(8,128)S(1)} %get-tuple-element.461), channel_id=1, source_target_pairs={{1,0},{3,2},{5,4},{7,6},{9,8},{11,10},{13,12},{15,14},{17,16},{19,... | collective-permute-start | bytes 28808 | tf_op jit(solution)/shard_map/ppermute | solution.py:41
  59.0 0.9 copy-start.3
  59.0 0.9 copy-start.7
  59.1 1.7 %copy-start = (f32[40,34,129]{0,2,1:T(8,128)S(1)}, f32[40,34,129]{0,2,1:T(8,128)}, u32[]{:S(2)}) copy-start(f32[40,34,129]{0,2,1:T(8,128)} %get-tuple-element.434) | copy-start | bytes 2105284
  67.4 1.1 %copy-start.1 = (f32[40,33,128]{2,1,0:T(8,128)S(1)}, f32[40,33,128]{2,1,0:T(8,128)}, u32[]{:S(2)}) copy-start(f32[40,33,128]{2,1,0:T(8,128)} %get-tuple-element.161) | copy-start | bytes 2027524 | tf_op jit(solution)/shard_map/cond
  67.4 1.4 %copy-start.2 = (f32[40,33,128]{2,1,0:T(8,128)S(1)}, f32[40,33,128]{2,1,0:T(8,128)}, u32[]{:S(2)}) copy-start(f32[40,33,128]{2,1,0:T(8,128)} %get-tuple-element.160) | copy-start | bytes 2027524 | tf_op jit(solution)/shard_map/cond
  74.5 4.8 %collective-permute-start.15 = (f32[1,32,128]{2,1,0:T(8,128)}, f32[1,32,128]{2,1,0:T(8,128)S(1)}, u32[]{:S(2)}, u32[]{:S(2)}) collective-permute-start(f32[1,32,128]{2,1,0:T(8,128)} %get-tuple-element.171), channel_id=1, source_target_pairs={{0,8},{8,16},{16,24},{24,0},{1,9},{9,17},{17,25},{25,1},{2,10},{10... | collective-permute-start | bytes 49160 | tf_op jit(solution)/shard_map/ppermute | solution.py:25
  79.3 4.6 %collective-permute-start.16 = (f32[1,32,128]{2,1,0:T(8,128)S(1)}, f32[1,32,128]{2,1,0:T(8,128)S(1)}, u32[]{:S(2)}, u32[]{:S(2)}) collective-permute-start(f32[1,32,128]{2,1,0:T(8,128)S(1)} %collective-permute-done.15), channel_id=1, source_target_pairs={{0,8},{8,16},{16,24},{24,0},{1,9},{9,17},{17,25},{25,1},{2,10},{10... | collective-permute-start | bytes 49160 | tf_op jit(solution)/shard_map/ppermute | solution.py:25
  84.0 4.6 %collective-permute-start.17 = (f32[1,32,128]{2,1,0:T(8,128)S(1)}, f32[1,32,128]{2,1,0:T(8,128)S(1)}, u32[]{:S(2)}, u32[]{:S(2)}) collective-permute-start(f32[1,32,128]{2,1,0:T(8,128)S(1)} %collective-permute-done.16), channel_id=1, source_target_pairs={{0,8},{8,16},{16,24},{24,0},{1,9},{9,17},{17,25},{25,1},{2,10},{10... | collective-permute-start | bytes 49160 | tf_op jit(solution)/shard_map/ppermute | solution.py:25
  89.4 5.0 %collective-permute-start.18 = (f32[5,3,4,128]{3,2,1,0:T(4,128)S(1)}, f32[5,3,4,128]{3,2,1,0:T(4,128)S(1)}, u32[]{:S(2)}, u32[]{:S(2)}) collective-permute-start(f32[5,3,4,128]{3,2,1,0:T(4,128)S(1)} %get-tuple-element.462), channel_id=1, source_target_pairs={{0,2},{2,4},{4,6},{1,3},{3,5},{5,7},{8,10},{10,12},{12,14},{9,11},... | collective-permute-start | bytes 92168 | tf_op jit(solution)/shard_map/ppermute | solution.py:39
  92.9 5.8 %collective-permute-start.19 = (f32[5,3,4,128]{3,2,1,0:T(4,128)S(1)}, f32[5,3,4,128]{3,2,1,0:T(4,128)S(1)}, u32[]{:S(2)}, u32[]{:S(2)}) collective-permute-start(f32[5,3,4,128]{3,2,1,0:T(4,128)S(1)} %get-tuple-element.463), channel_id=1, source_target_pairs={{2,0},{4,2},{6,4},{3,1},{5,3},{7,5},{10,8},{12,10},{14,12},{11,9},... | collective-permute-start | bytes 92168 | tf_op jit(solution)/shard_map/ppermute | solution.py:41
  98.9 2.6 %collective-permute-start.20 = (f32[5,3,40,4]{3,2,1,0:T(8,128)S(1)}, f32[5,3,40,4]{3,2,1,0:T(8,128)S(1)}, u32[]{:S(2)}, u32[]{:S(2)}) collective-permute-start(f32[5,3,40,4]{3,2,1,0:T(8,128)S(1)} %get-tuple-element.458), channel_id=1, source_target_pairs={{0,1},{2,3},{4,5},{6,7},{8,9},{10,11},{12,13},{14,15},{16,17},{18,... | collective-permute-start | bytes 28808 | tf_op jit(solution)/shard_map/ppermute | solution.py:39
  100.2 3.5 %collective-permute-start.21 = (f32[5,3,40,4]{3,2,1,0:T(8,128)S(1)}, f32[5,3,40,4]{3,2,1,0:T(8,128)S(1)}, u32[]{:S(2)}, u32[]{:S(2)}) collective-permute-start(f32[5,3,40,4]{3,2,1,0:T(8,128)S(1)} %get-tuple-element.459), channel_id=1, source_target_pairs={{1,0},{3,2},{5,4},{7,6},{9,8},{11,10},{13,12},{15,14},{17,16},{19,... | collective-permute-start | bytes 28808 | tf_op jit(solution)/shard_map/ppermute | solution.py:41
